TPU v7x, 256 devices: a whole 4x4x8 slice. The times are simulated.
256 devices in a mesh: gx: 16 (over y, x), gy: 16 (over z, core).
Axes of the slice: x: 4, y: 4, z: 8, core: 2. Of those that a mesh axis runs over, the one named last changes fastest.
Arguments:
- state: float32 [1024, 6, 16, 16, 128], P(('gx', 'gy')), may hold values from -1 to 4, as said below
- metrics: bfloat16 [1024, 10, 16, 16, 128], P(('gx', 'gy')), may hold values from -0.3 to 1.4, as said below
- nbr_block: int32 [1024, 4], P(('gx', 'gy')), may hold values from 0 to 1023, as said below
- nbr_face: int32 [1024, 4], P(('gx', 'gy')), may hold values from 0 to 3
- flip: int32 [1024, 4], P(('gx', 'gy')), may hold values from 0 to 1
- bc_code: int32 [1024, 4], P(('gx', 'gy')), may hold values from 0 to 3
Outputs:
- new_state: float32 [1024, 6, 16, 16, 128], P(('gx', 'gy'))
- residual: float32 [1024, 6, 16, 16, 128], P(('gx', 'gy'))
Inputs may be any that keep to these rules, and one draw needn't show every extreme that they name: `nbr_block`: an interface face's neighbour block lies on the same device or on a device whose index differs by one along exactly one of gx and gy. Connectivity is mutual: if face f of block b meets face f2 of block b2, then face f2 of b2 meets face f of b with the same flip. Faces with bc_code other than 0 name their own block and face with flip 0. The faces of one device's blocks meet at most 4 faces of blocks of a device beside it along gy, and at most one face of blocks of a device beside it along gx; both bounds are reached. `state`: density and pressure are positive. `metrics`: volumes are positive.
All inputs are finite; a program needn't handle non-finite values.
Results may differ from a plain program's by a relative error of at most 0.0003.
Values sent between devices are 32-bit elements; how exact they have to be, the bound alone decides.
A program may use at most 64 MiB of HBM per device.

v0:
```python
import jax
import jax.numpy as jnp
from jax import lax
from jax.sharding import PartitionSpec as P

GAMMA = 1.4
GAMMA_MINUS = 0.4
VISCOSITY = 0.02
CFL_NUMBER = 0.5
CB_ONE = 0.1355
CW_ONE = 3.24


def shifted(value, axis, steps):
    count = lax.axis_size(axis)
    initial, last = (max(0, -steps), min(count, count - steps))
    return lax.ppermute(value, axis, [(source, source + steps) for source in range(initial, last)])


def wall_sign():
    return jnp.array([1.0, -1.0, -1.0, -1.0, 1.0, -1.0], jnp.float32)


def free_stream():
    return jnp.array([1.0, 0.5, 0.0, 0.1, 2.1325, 0.05], jnp.float32)


def euler_flux(cons, area):
    density = cons[0]
    velocity = cons[1:4] / density
    pressure = GAMMA_MINUS * (cons[4] - 0.5 * jnp.sum(cons[1:4] * velocity, axis=0))
    normal = jnp.sum(velocity * area, axis=0)
    sound = jnp.sqrt(GAMMA * jnp.abs(pressure) / density)
    flux = jnp.concatenate(
        [
            cons[0:1] * normal,
            cons[1:4] * normal + pressure * area,
            ((cons[4] + pressure) * normal)[None],
            (cons[5] * normal)[None],
        ],
        0,
    )
    speed = jnp.abs(normal) + sound * jnp.sqrt(jnp.sum(area * area, axis=0))
    return (flux, speed)


def face_average(values, axis):
    count = values.shape[axis]
    padded = jnp.concatenate(
        [
            lax.slice_in_dim(values, 0, 1, axis=axis),
            values,
            lax.slice_in_dim(values, count - 1, count, axis=axis),
        ],
        axis,
    )
    return 0.5 * (
        lax.slice_in_dim(padded, 0, count + 1, axis=axis)
        + lax.slice_in_dim(padded, 1, count + 2, axis=axis)
    )


def flux_balance(padded, normals, volume, axis):
    count = normals.shape[axis]
    area = face_average(normals, axis)
    face_volume = face_average(volume, axis - 1)
    left = lax.slice_in_dim(padded, 0, count + 1, axis=axis)
    right = lax.slice_in_dim(padded, 1, count + 2, axis=axis)
    flux_left, speed_left = euler_flux(left, area)
    flux_right, speed_right = euler_flux(right, area)
    jump = right - left
    flux = 0.5 * (flux_left + flux_right) - 0.5 * jnp.maximum(speed_left, speed_right) * jump
    eddy = 0.5 * (left[5] / left[0] + right[5] / right[0])
    coeff = (VISCOSITY + eddy) * jnp.sum(area * area, axis=0) / face_volume
    viscous = jnp.concatenate([jnp.zeros_like(jump[0:1]), coeff * jump[1:]], 0)
    flux = flux - viscous
    return lax.slice_in_dim(flux, 1, count + 1, axis=axis) - lax.slice_in_dim(
        flux, 0, count, axis=axis
    )


def velocity_change(padded, axis):
    count = padded.shape[axis] - 2
    velocity = padded[1:4] / padded[0]
    return 0.5 * (
        lax.slice_in_dim(velocity, 2, count + 2, axis=axis)
        - lax.slice_in_dim(velocity, 0, count, axis=axis)
    )


def block_residual(cells, halos, metric):
    length = cells.shape[3]
    geometry = metric.astype(jnp.float32)
    normal_i, normal_j, normal_k, volume = (
        geometry[0:3],
        geometry[3:6],
        geometry[6:9],
        geometry[9],
    )
    along_i = jnp.concatenate([halos[0][:, None], cells, halos[1][:, None]], 1)
    along_j = jnp.concatenate([halos[2][:, :, None], cells, halos[3][:, :, None]], 2)
    wall = cells[:, :, :, 0:1] * wall_sign()[:, None, None, None]
    freely = jnp.broadcast_to(free_stream()[:, None, None, None], wall.shape)
    along_k = jnp.concatenate([wall, cells, freely], 3)
    balance = (
        flux_balance(along_i, normal_i, volume, 1)
        + flux_balance(along_j, normal_j, volume, 2)
        + flux_balance(along_k, normal_k, volume, 3)
    )
    tensor = (
        velocity_change(along_i, 1)[:, None] * normal_i[None]
        + velocity_change(along_j, 2)[:, None] * normal_j[None]
        + velocity_change(along_k, 3)[:, None] * normal_k[None]
    ) / volume
    vorticity = jnp.stack(
        [tensor[2, 1] - tensor[1, 2], tensor[0, 2] - tensor[2, 0], tensor[1, 0] - tensor[0, 1]], 0
    )
    omega = jnp.sqrt(jnp.sum(vorticity * vorticity, axis=0) + 0.0001)
    eddy = cells[5] / cells[0]
    distance = 1.0 + 4.0 * jnp.arange(length, dtype=jnp.float32) / length
    source = CB_ONE * omega * cells[5] - CW_ONE * cells[5] * eddy / (distance * distance)
    residual = balance / volume
    return jnp.concatenate([residual[0:5], (residual[5] - source)[None]], 0)


def time_limit(cells, metric):
    geometry = metric.astype(jnp.float32)
    total = (
        euler_flux(cells, geometry[0:3])[1]
        + euler_flux(cells, geometry[3:6])[1]
        + euler_flux(cells, geometry[6:9])[1]
    )
    return jnp.min(geometry[9] / total)


def face_layers(cells):
    return jnp.stack([cells[:, 0], cells[:, -1], cells[:, :, 0], cells[:, :, -1]], 0)


def boundary_halo(fetched, own, flip, bc_code):
    turned = jnp.where(flip[..., None, None, None] == 1, jnp.flip(fetched, -2), fetched)
    wall = own * wall_sign()[:, None, None]
    freely = jnp.broadcast_to(free_stream()[:, None, None], own.shape)
    code = bc_code[..., None, None, None]
    return jnp.where(
        code == 0, turned, jnp.where(code == 1, wall, jnp.where(code == 2, freely, own))
    )


def slot_of(marked, keys):
    same = marked[:, None] & marked[None, :]
    return jnp.sum(same & (keys[None, :] < keys[:, None]), axis=1)


def per_device(state, metrics, nbr_block, nbr_face, flip, bc_code):
    blocks = state.shape[0]
    groups = lax.axis_size("gy")
    grid_col = lax.axis_index("gy")
    grid_row = lax.axis_index("gx")
    partner = nbr_block.reshape(-1)
    facing = nbr_face.reshape(-1)
    interface = bc_code.reshape(-1) == 0
    far_device = partner // blocks
    far_row = far_device // groups
    far_col = far_device % groups
    own_key = jnp.arange(partner.shape[0], dtype=jnp.int32)
    far_key = partner % blocks * 4 + facing

    def toward(step_row, step_col):
        return interface & (far_row == grid_row + step_row) & (far_col == grid_col + step_col)

    def plan(step_row, step_col):
        sending = toward(step_row, step_col)
        taking = toward(-step_row, -step_col)
        return (sending, slot_of(sending, own_key), taking, slot_of(taking, far_key))

    row_plans = [plan(1, 0), plan(-1, 0)]
    col_plans = [plan(0, 1), plan(0, -1)]

    def pack(flat, sending, send_slot, capacity):
        outgoing = jnp.zeros((capacity,) + flat.shape[1:], jnp.float32)
        return outgoing.at[jnp.where(sending, send_slot, capacity)].set(flat, mode="drop")

    def halos_for(cells):
        layers = jax.vmap(face_layers)(cells)
        flat = layers.reshape((blocks * 4,) + layers.shape[2:])
        fetched = flat[far_key]
        for offset, entry in zip((1, -1), row_plans):
            outgoing = pack(flat, entry[0], entry[1], 1)
            incoming = shifted(outgoing, "gx", offset)
            fetched = jnp.where(
                entry[2][:, None, None, None], incoming[jnp.minimum(entry[3], 0)], fetched
            )
        for offset, entry in zip((1, -1), col_plans):
            outgoing = pack(flat, entry[0], entry[1], blocks)
            incoming = shifted(outgoing, "gy", offset)
            fetched = jnp.where(
                entry[2][:, None, None, None], incoming[jnp.minimum(entry[3], blocks - 1)], fetched
            )
        fetched = fetched.reshape(layers.shape)
        return boundary_halo(fetched, layers, flip, bc_code)

    def residual_local(cells):
        halos = halos_for(cells)
        return lax.map(
            lambda operands: block_residual(operands[0], operands[1], operands[2]),
            (cells, halos, metrics),
        )

    limits = lax.map(lambda operands: time_limit(operands[0], operands[1]), (state, metrics))
    step = CFL_NUMBER * lax.pmin(jnp.min(limits), ("gx", "gy"))
    first = residual_local(state)
    middle = state - 0.5 * step * first
    second = residual_local(middle)
    return (state - step * second, second)


def solution(mesh):
    return jax.shard_map(
        per_device,
        mesh=mesh,
        in_specs=(
            P(("gx", "gy"), None, None, None, None),
            P(("gx", "gy"), None, None, None, None),
            P(("gx", "gy"), None),
            P(("gx", "gy"), None),
            P(("gx", "gy"), None),
            P(("gx", "gy"), None),
        ),
        out_specs=(
            P(("gx", "gy"), None, None, None, None),
            P(("gx", "gy"), None, None, None, None),
        ),
        check_vma=False,
    )
```

profile of v0, /device:TPU:40, one launch (start us, length us, event | category | flops | bytes accessed | tf_op | source)
XLA Modules:
  0.0 314.5 jit_solution(8675506350946782071)
XLA Ops:
  5.1 2.9 copy.108
  11.5 1.9 collective-permute-start
  14.2 3.2 %scatter_fusion.1 = f32[4,6,16,128]{3,2,1,0:T(8,128)} fusion(f32[4,6,16,128]{3,2,1,0:T(8,128)} %broadcast.2355.clone.2, s32[16]{0:T(128)S(1)} %get-tuple-element.496, f32[16,6,16,128]{3,2,1,0:T(8,128)S(1)} %bitcast.1020), kind=kCustom, calls=%fused_computation.7 | custom fusion | bytes 2359360 | tf_op jit(solution)/shard_map/scatter | solution.py:182
  17.3 2.4 collective-permute-start.1
  20.9 3.4 %collective-permute-start.3 = (f32[1,6,16,128]{3,2,1,0:T(8,128)S(1)}, f32[1,6,16,128]{3,2,1,0:T(8,128)S(1)}, u32[]{:S(2)}, u32[]{:S(2)}) collective-permute-start(f32[1,6,16,128]{3,2,1,0:T(8,128)S(1)} %bitcast.1031), channel_id=1, source_target_pairs={{0,16},{16,32},{32,48},{48,64},{64,80},{80,96},{96,112},{112,128},... | collective-permute-start | bytes 147464 | tf_op jit(solution)/shard_map/ppermute | solution.py:17
  25.4 4.6 %collective-permute-start.2 = (f32[1,6,16,128]{3,2,1,0:T(8,128)S(1)}, f32[1,6,16,128]{3,2,1,0:T(8,128)S(1)}, u32[]{:S(2)}, u32[]{:S(2)}) collective-permute-start(f32[1,6,16,128]{3,2,1,0:T(8,128)S(1)} %bitcast.1032), channel_id=1, source_target_pairs={{16,0},{32,16},{48,32},{64,48},{80,64},{96,80},{112,96},{128,112},... | collective-permute-start | bytes 147464 | tf_op jit(solution)/shard_map/ppermute | solution.py:17
  32.3 26.6 %while.36 = (s32[]{:T(128)}, f32[4]{0:T(128)}, bf16[4,10,16,16,128]{4,3,2,1,0:T(8,128)(2,1)}, f32[4,6,16,16,128]{4,3,2,1,0:T(8,128)}, s32[]{:T(128)}, /*index=5*/s32[]{:T(128)}, s32[]{}, s32[]{}) while((s32[]{:T(128)}, f32[4]{0:T(128)}, bf16[4,10,16,16,128]{4,3,2,1,0:T(8,128)(2,1)}, f32[4,6,16,16,128]{4,3,2,1,0:T(8,128)}, s32[]{:T(128)}, ...), condition=%wide.region_9.10_spmd, body=%wide.region_0.9_spmd.sunk | while | flops 2195459 | bytes 6160717 | solution.py:210
  35.7 1.9 fusion.273
  42.4 1.9 fusion.273
  49.0 1.9 fusion.273
  55.7 1.9 fusion.273
  61.4 77.9 %pmin.7 = f32[]{:T(128)} all-reduce(f32[]{:T(128)} %reduce_min.18), channel_id=1, replica_groups=mesh['gx'=16,'gy'=16] {'gx','gy'}, use_global_device_ids=true, to_apply=%region_11.12 | all-reduce | flops 1 | bytes 8 | tf_op jit(solution)/shard_map/pmin | solution.py:211
  140.7 1.5 gather_fusion
  142.2 1.5 gather_fusion.1
  146.7 65.9 %while.37 = (s32[]{:T(128)}, f32[4,6,16,16,128]{4,2,1,0,3:T(8,128)}, f32[4,4,6,16,128]{4,3,2,1,0:T(8,128)}, f32[4,6,16,16,128]{4,3,2,1,0:T(8,128)}, bf16[4,10,16...) while((s32[]{:T(128)}, ...), condition=%wide.region_41.42_spmd.clone, body=%wide.region_24.41_spmd.sunk.clone.sunk | while | flops 34659460 | bytes 94720760 | solution.py:205
  150.6 1.4 dynamic-slice_convert_fusion.7
  167.1 1.4 dynamic-slice_convert_fusion.7
  183.6 1.4 dynamic-slice_convert_fusion.7
  200.0 1.4 dynamic-slice_convert_fusion.7
  212.5 5.6 %multiply_subtract_fusion.1 = f32[4,6,16,16,128]{4,2,1,0,3:T(8,128)} fusion(f32[4,6,16,16,128]{4,2,1,0,3:T(8,128)} %get-tuple-element.203, f32[]{:T(128)S(6)} %mul.2232, f32[4,6,16,16,128]{4,3,2,1,0:T(8,128)} %param.20), kind=kLoop, calls=%fused_computation.560 | loop fusion | flops 1572864 | bytes 9437188 | tf_op jit(solution)/shard_map/sub | solution.py:213
  218.1 2.2 fusion.222
  223.3 1.9 collective-permute-start.5
  226.4 3.6 %collective-permute-start.4 = (f32[4,6,16,128]{3,2,1,0:T(8,128)S(1)}, f32[4,6,16,128]{3,2,1,0:T(8,128)S(1)}, u32[]{:S(2)}, u32[]{:S(2)}) collective-permute-start(f32[4,6,16,128]{3,2,1,0:T(8,128)S(1)} %scatter_fusion.4), channel_id=1, source_target_pairs={{1,0},{2,1},{3,2},{4,3},{5,4},{6,5},{7,6},{8,7},{9,8},{10,9},{11,1... | collective-permute-start | bytes 589832 | tf_op jit(solution)/shard_map/ppermute | solution.py:17
  231.2 1.9 collective-permute-start.7
  234.2 6.0 %collective-permute-start.6 = (f32[1,6,16,128]{3,2,1,0:T(8,128)S(1)}, f32[1,6,16,128]{3,2,1,0:T(8,128)S(1)}, u32[]{:S(2)}, u32[]{:S(2)}) collective-permute-start(f32[1,6,16,128]{3,2,1,0:T(8,128)S(1)} %bitcast.1029), channel_id=1, source_target_pairs={{16,0},{32,16},{48,32},{64,48},{80,64},{96,80},{112,96},{128,112},... | collective-permute-start | bytes 147464 | tf_op jit(solution)/shard_map/ppermute | solution.py:17
  245.3 1.3 fusion.183
  246.6 62.9 %while.38 = (s32[]{:T(128)}, f32[4,6,16,16,128]{4,3,2,1,0:T(8,128)}, f32[4,4,6,16,128]{4,3,2,1,0:T(8,128)}, f32[4,6,16,16,128]{4,2,1,0,3:T(8,128)}, bf16[4,10,16...) while((s32[]{:T(128)}, ...), condition=%wide.region_63.64_spmd.clone, body=%wide.region_46.63_spmd.sunk.clone.sunk | while | flops 34659460 | bytes 94720736 | solution.py:205
  251.0 1.4 dynamic-slice_convert_fusion.8
  266.8 1.4 dynamic-slice_convert_fusion.8
  282.5 1.4 dynamic-slice_convert_fusion.8
  298.2 1.4 dynamic-slice_convert_fusion.8
  309.5 5.0 %multiply_subtract_fusion = f32[4,6,16,16,128]{4,3,2,1,0:T(8,128)} fusion(f32[4,6,16,16,128]{4,3,2,1,0:T(8,128)} %param.20, f32[4,6,16,16,128]{4,3,2,1,0:T(8,128)} %get-tuple-element.201, f32[]{:T(128)S(6)} %mul.2230), kind=kLoop, calls=%fused_computation.559 | loop fusion | flops 1572864 | bytes 9437188 | tf_op jit(solution)/shard_map/sub | solution.py:215
  (663 shorter events, 163.6 us)
Async XLA Ops:
  2.6 141.8 %copy-start.16 = (pred[4,4]{1,0:T(4,128)(4,1)}, pred[4,4]{1,0:T(4,128)(4,1)S(1)}, u32[]{:S(2)}) copy-start(pred[4,4]{1,0:T(4,128)(4,1)S(1)} %get-tuple-element.353) | copy-start | bytes 52
  2.6 141.8 %copy-start.21 = (pred[4,4]{1,0:T(4,128)(4,1)}, pred[4,4]{1,0:T(4,128)(4,1)S(1)}, u32[]{:S(2)}) copy-start(pred[4,4]{1,0:T(4,128)(4,1)S(1)} %get-tuple-element.490) | copy-start | bytes 52
  2.6 141.8 %copy-start.23 = (pred[4,4]{1,0:T(4,128)(4,1)}, pred[4,4]{1,0:T(4,128)(4,1)S(1)}, u32[]{:S(2)}) copy-start(pred[4,4]{1,0:T(4,128)(4,1)S(1)} %get-tuple-element.491) | copy-start | bytes 52
  10.0 14.4 %copy-start.33 = (s32[16]{0:T(128)}, s32[16]{0:T(128)S(1)}, u32[]{:S(2)}) copy-start(s32[16]{0:T(128)S(1)} %get-tuple-element.356) | copy-start | bytes 196
  10.3 3.9 %copy-start.29 = (s32[16]{0:T(128)}, s32[16]{0:T(128)S(1)}, u32[]{:S(2)}) copy-start(s32[16]{0:T(128)S(1)} %get-tuple-element.496) | copy-start | bytes 196
  11.5 129.1 %collective-permute-start = (f32[4,6,16,128]{3,2,1,0:T(8,128)S(1)}, f32[4,6,16,128]{3,2,1,0:T(8,128)}, u32[]{:S(2)}, u32[]{:S(2)}) collective-permute-start(f32[4,6,16,128]{3,2,1,0:T(8,128)S(1)} %scatter_fusion), channel_id=1, source_target_pairs={{1,0},{2,1},{3,2},{4,3},{5,4},{6,5},{7,6},{8,7},{9,8},{10,9},{11,1... | collective-permute-start | bytes 589832 | tf_op jit(solution)/shard_map/ppermute | solution.py:17
  17.3 124.9 %collective-permute-start.1 = (f32[4,6,16,128]{3,2,1,0:T(8,128)}, f32[4,6,16,128]{3,2,1,0:T(8,128)}, u32[]{:S(2)}, u32[]{:S(2)}) collective-permute-start(f32[4,6,16,128]{3,2,1,0:T(8,128)} %scatter_fusion.1), channel_id=1, source_target_pairs={{0,1},{1,2},{2,3},{3,4},{4,5},{5,6},{6,7},{7,8},{8,9},{9,10},{10,1... | collective-permute-start | bytes 589832 | tf_op jit(solution)/shard_map/ppermute | solution.py:17
  19.8 5.7 %copy-start.31 = (s32[16]{0:T(128)}, s32[16]{0:T(128)S(1)}, u32[]{:S(2)}) copy-start(s32[16]{0:T(128)S(1)} %fusion.196) | copy-start | bytes 196
  20.9 10.8 %copy-start.41 = (s32[4,4]{1,0:T(4,128)S(1)}, s32[4,4]{1,0:T(4,128)}, u32[]{:S(2)}) copy-start(s32[4,4]{1,0:T(4,128)} %param.24) | copy-start | bytes 196
  20.9 122.9 %collective-permute-start.3 = (f32[1,6,16,128]{3,2,1,0:T(8,128)S(1)}, f32[1,6,16,128]{3,2,1,0:T(8,128)S(1)}, u32[]{:S(2)}, u32[]{:S(2)}) collective-permute-start(f32[1,6,16,128]{3,2,1,0:T(8,128)S(1)} %bitcast.1031), channel_id=1, source_target_pairs={{0,16},{16,32},{32,48},{48,64},{64,80},{80,96},{96,112},{112,128},... | collective-permute-start | bytes 147464 | tf_op jit(solution)/shard_map/ppermute | solution.py:17
  25.4 118.3 %collective-permute-start.2 = (f32[1,6,16,128]{3,2,1,0:T(8,128)S(1)}, f32[1,6,16,128]{3,2,1,0:T(8,128)S(1)}, u32[]{:S(2)}, u32[]{:S(2)}) collective-permute-start(f32[1,6,16,128]{3,2,1,0:T(8,128)S(1)} %bitcast.1032), channel_id=1, source_target_pairs={{16,0},{32,16},{48,32},{64,48},{80,64},{96,80},{112,96},{128,112},... | collective-permute-start | bytes 147464 | tf_op jit(solution)/shard_map/ppermute | solution.py:17
  30.0 110.6 %copy-start.18 = (s32[1024]{0:T(1024)}, s32[1024]{0:T(1024)S(1)}, u32[]{:S(2)}) copy-start(s32[1024]{0:T(1024)S(1)} %pad_clamp_fusion.2) | copy-start | bytes 12292
  35.7 1.9 copy-start.42
  42.4 1.9 copy-start.42
  49.0 1.9 copy-start.42
  55.7 1.9 copy-start.42
  60.8 81.4 %copy-start.19 = (s32[1024]{0:T(1024)}, s32[1024]{0:T(1024)S(1)}, u32[]{:S(2)}) copy-start(s32[1024]{0:T(1024)S(1)} %pad_clamp_fusion.1) | copy-start | bytes 12292
  61.4 80.8 %copy-start.20 = (s32[1024]{0:T(1024)}, s32[1024]{0:T(1024)S(1)}, u32[]{:S(2)}) copy-start(s32[1024]{0:T(1024)S(1)} %pad_clamp_fusion) | copy-start | bytes 12292
  140.6 3.2 %copy-start.35 = (pred[4,4]{1,0:T(4,128)(4,1)S(1)}, pred[4,4]{1,0:T(4,128)(4,1)}, u32[]{:S(2)}) copy-start(pred[4,4]{1,0:T(4,128)(4,1)} %get-tuple-element.349) | copy-start | bytes 52
  140.6 3.2 %copy-start.37 = (pred[4,4]{1,0:T(4,128)(4,1)S(1)}, pred[4,4]{1,0:T(4,128)(4,1)}, u32[]{:S(2)}) copy-start(pred[4,4]{1,0:T(4,128)(4,1)} %get-tuple-element.354) | copy-start | bytes 52
  140.6 3.2 %copy-start.39 = (pred[4,4]{1,0:T(4,128)(4,1)S(1)}, pred[4,4]{1,0:T(4,128)(4,1)}, u32[]{:S(2)}) copy-start(pred[4,4]{1,0:T(4,128)(4,1)} %get-tuple-element.492) | copy-start | bytes 52
  140.6 3.2 %copy-start.40 = (pred[4,4]{1,0:T(4,128)(4,1)S(1)}, pred[4,4]{1,0:T(4,128)(4,1)}, u32[]{:S(2)}) copy-start(pred[4,4]{1,0:T(4,128)(4,1)} %and_and_fusion.2) | copy-start | bytes 52
  221.3 2.0 copy-start.10
  222.2 3.1 copy-start.28
  223.3 6.8 %copy-start.32 = (s32[16]{0:T(128)S(1)}, s32[16]{0:T(128)}, u32[]{:S(2)}) copy-start(s32[16]{0:T(128)} %copy-done.31) | copy-start | bytes 196
  223.3 18.3 %collective-permute-start.5 = (f32[4,6,16,128]{3,2,1,0:T(8,128)S(1)}, f32[4,6,16,128]{3,2,1,0:T(8,128)S(1)}, u32[]{:S(2)}, u32[]{:S(2)}) collective-permute-start(f32[4,6,16,128]{3,2,1,0:T(8,128)S(1)} %scatter_fusion.5), channel_id=1, source_target_pairs={{0,1},{1,2},{2,3},{3,4},{4,5},{5,6},{6,7},{7,8},{8,9},{9,10},{10,1... | collective-permute-start | bytes 589832 | tf_op jit(solution)/shard_map/ppermute | solution.py:17
  226.4 6.7 %copy-start.34 = (s32[16]{0:T(128)S(1)}, s32[16]{0:T(128)}, u32[]{:S(2)}) copy-start(s32[16]{0:T(128)} %copy-done.33) | copy-start | bytes 196
  226.4 16.0 %collective-permute-start.4 = (f32[4,6,16,128]{3,2,1,0:T(8,128)S(1)}, f32[4,6,16,128]{3,2,1,0:T(8,128)S(1)}, u32[]{:S(2)}, u32[]{:S(2)}) collective-permute-start(f32[4,6,16,128]{3,2,1,0:T(8,128)S(1)} %scatter_fusion.4), channel_id=1, source_target_pairs={{1,0},{2,1},{3,2},{4,3},{5,4},{6,5},{7,6},{8,7},{9,8},{10,9},{11,1... | collective-permute-start | bytes 589832 | tf_op jit(solution)/shard_map/ppermute | solution.py:17
  231.2 12.0 %collective-permute-start.7 = (f32[1,6,16,128]{3,2,1,0:T(8,128)S(1)}, f32[1,6,16,128]{3,2,1,0:T(8,128)S(1)}, u32[]{:S(2)}, u32[]{:S(2)}) collective-permute-start(f32[1,6,16,128]{3,2,1,0:T(8,128)S(1)} %bitcast.1030), channel_id=1, source_target_pairs={{0,16},{16,32},{32,48},{48,64},{64,80},{80,96},{96,112},{112,128},... | collective-permute-start | bytes 147464 | tf_op jit(solution)/shard_map/ppermute | solution.py:17
  234.2 8.9 %collective-permute-start.6 = (f32[1,6,16,128]{3,2,1,0:T(8,128)S(1)}, f32[1,6,16,128]{3,2,1,0:T(8,128)S(1)}, u32[]{:S(2)}, u32[]{:S(2)}) collective-permute-start(f32[1,6,16,128]{3,2,1,0:T(8,128)S(1)} %bitcast.1029), channel_id=1, source_target_pairs={{16,0},{32,16},{48,32},{64,48},{80,64},{96,80},{112,96},{128,112},... | collective-permute-start | bytes 147464 | tf_op jit(solution)/shard_map/ppermute | solution.py:17
  241.6 1.5 copy-start.36
  241.7 1.5 copy-start.38
  (26 other events, 25.5 us)
where the time goes:
time: 318 us; the launch traced here: 315 us
  other arithmetic  138 us (43%)
  blocking collectives  77.9 us (24%)
  local copies, waits for them, and re-layouts  67.5 us (21%)
  starting transfers between devices  25.8 us (8%)
    pmin x1, blocking collectives, per_device(): step = CFL_NUMBER * lax.pmin(jnp.min(limits), ('gx', 'gy'))  77.9 us
    ppermute x8, starting transfers between devices, shifted(): lax.ppermute(value, axis, [(source, source + steps) for source in range(i...  25.8 us
    reduce_sum x28, other arithmetic, euler_flux(): normal = jnp.sum(velocity * area, axis=0)  16.6 us
    sub x24, other arithmetic, flux_balance(): flux = flux - viscous  13.4 us
    convert_element_type x8, other arithmetic, block_residual(): geometry = metric.astype(jnp.float32)  10.9 us
    scatter x8, local copies, waits for them, and re-layouts, pack(): outgoing.at[jnp.where(sending, send_slot, capacity)].set(flat, mode='drop')  10.9 us
    mul x24, other arithmetic, flux_balance(): 0.5 * jnp.maximum(speed_left, speed_right) * jump  9.22 us
    reduce_min x4, other arithmetic, time_limit(): return jnp.min(geometry[9] / total)  7.44 us
  transfers between devices with their start and end apart: 8, of which 0 were waited for; matrix products, arithmetic and copies ran while one was open for 14% of the time, Pallas kernels for 0%

commit v1 on v0

--- a/solution.py
+++ b/solution.py
@@ -208,7 +208,7 @@
         )
 
     limits = lax.map(lambda operands: time_limit(operands[0], operands[1]), (state, metrics))
-    step = CFL_NUMBER * lax.pmin(jnp.min(limits), ("gx", "gy"))
+    step = CFL_NUMBER * lax.pmin(lax.pmin(jnp.min(limits), "gy"), "gx")
     first = residual_local(state)
     middle = state - 0.5 * step * first
     second = residual_local(middle)

time: 318 us -> 303 us (0.953)
  the two profiles are of different devices: /device:TPU:40 before, /device:TPU:128 now
where the time goes in v1:
time: 303 us; the launch traced here: 300 us
  other arithmetic  138 us (46%)
  blocking collectives  68.4 us (23%)
  local copies, waits for them, and re-layouts  67.5 us (22%)
  starting transfers between devices  18.4 us (6%)
    pmin x2, blocking collectives, per_device(): step = CFL_NUMBER * lax.pmin(lax.pmin(jnp.min(limits), 'gy'), 'gx')  68.4 us
    ppermute x8, starting transfers between devices, shifted(): lax.ppermute(value, axis, [(source, source + steps) for source in range(i...  18.4 us
    reduce_sum x28, other arithmetic, euler_flux(): normal = jnp.sum(velocity * area, axis=0)  16.6 us
    sub x24, other arithmetic, flux_balance(): flux = flux - viscous  13.4 us
    convert_element_type x8, other arithmetic, block_residual(): geometry = metric.astype(jnp.float32)  10.9 us
    scatter x8, local copies, waits for them, and re-layouts, pack(): outgoing.at[jnp.where(sending, send_slot, capacity)].set(flat, mode='drop')  10.8 us
    mul x24, other arithmetic, flux_balance(): 0.5 * jnp.maximum(speed_left, speed_right) * jump  9.22 us
    reduce_min x4, other arithmetic, time_limit(): return jnp.min(geometry[9] / total)  7.44 us
  transfers between devices with their start and end apart: 8, of which 1 were waited for; matrix products, arithmetic and copies ran while one was open for 15% of the time, Pallas kernels for 0%

profile of v1, /device:TPU:128, one launch (start us, length us, event | category | flops | bytes accessed | tf_op | source)
XLA Modules:
  0.0 300.0 jit_solution(8666420498574545809)
XLA Ops:
  5.1 2.9 copy.108
  11.5 1.9 collective-permute-start
  14.2 3.2 %scatter_fusion.1 = f32[4,6,16,128]{3,2,1,0:T(8,128)} fusion(f32[4,6,16,128]{3,2,1,0:T(8,128)} %broadcast.2355.clone.2, s32[16]{0:T(128)S(1)} %get-tuple-element.496, f32[16,6,16,128]{3,2,1,0:T(8,128)S(1)} %bitcast.1020), kind=kCustom, calls=%fused_computation.7 | custom fusion | bytes 2359360 | tf_op jit(solution)/shard_map/scatter | solution.py:182
  17.4 2.4 collective-permute-start.1
  20.9 3.4 %collective-permute-start.3 = (f32[1,6,16,128]{3,2,1,0:T(8,128)S(1)}, f32[1,6,16,128]{3,2,1,0:T(8,128)S(1)}, u32[]{:S(2)}, u32[]{:S(2)}) collective-permute-start(f32[1,6,16,128]{3,2,1,0:T(8,128)S(1)} %bitcast.1031), channel_id=1, source_target_pairs={{0,16},{16,32},{32,48},{48,64},{64,80},{80,96},{96,112},{112,128},... | collective-permute-start | bytes 147464 | tf_op jit(solution)/shard_map/ppermute | solution.py:17
  29.0 26.6 %while.36 = (s32[]{:T(128)}, f32[4]{0:T(128)}, bf16[4,10,16,16,128]{4,3,2,1,0:T(8,128)(2,1)}, f32[4,6,16,16,128]{4,3,2,1,0:T(8,128)}, s32[]{:T(128)}, /*index=5*/s32[]{:T(128)}, s32[]{}, s32[]{}) while((s32[]{:T(128)}, f32[4]{0:T(128)}, bf16[4,10,16,16,128]{4,3,2,1,0:T(8,128)(2,1)}, f32[4,6,16,16,128]{4,3,2,1,0:T(8,128)}, s32[]{:T(128)}, ...), condition=%wide.region_9.10_spmd, body=%wide.region_0.9_spmd.sunk | while | flops 2195459 | bytes 6160717 | solution.py:210
  32.5 1.9 fusion.273
  39.1 1.9 fusion.273
  45.8 1.9 fusion.273
  52.4 1.9 fusion.273
  57.5 26.2 %pmin.14 = f32[]{:T(128)} all-reduce(f32[]{:T(128)} %reduce_min.18), channel_id=1, replica_groups=mesh['gx'=16,'gy'=16] {'gy'}, use_global_device_ids=true, to_apply=%region_11.12 | all-reduce | flops 1 | bytes 8 | tf_op jit(solution)/shard_map/pmin | solution.py:211
  85.0 42.2 %pmin.15 = f32[]{:T(128)} all-reduce(f32[]{:T(128)} %pmin.14), channel_id=1, replica_groups=mesh['gx'=16,'gy'=16] {'gx'}, use_global_device_ids=true, to_apply=%region_12.13 | all-reduce | flops 1 | bytes 8 | tf_op jit(solution)/shard_map/pmin | solution.py:211
  128.5 1.5 gather_fusion
  130.1 1.5 gather_fusion.1
  133.2 1.3 fusion.185
  134.6 65.9 %while.37 = (s32[]{:T(128)}, f32[4,6,16,16,128]{4,2,1,0,3:T(8,128)}, f32[4,4,6,16,128]{4,3,2,1,0:T(8,128)}, f32[4,6,16,16,128]{4,3,2,1,0:T(8,128)}, bf16[4,10,16...) while((s32[]{:T(128)}, ...), condition=%wide.region_42.43_spmd.clone, body=%wide.region_25.42_spmd.sunk.clone.sunk | while | flops 34659460 | bytes 94720760 | solution.py:205
  138.5 1.4 dynamic-slice_convert_fusion.7
  155.0 1.4 dynamic-slice_convert_fusion.7
  171.5 1.4 dynamic-slice_convert_fusion.7
  187.9 1.4 dynamic-slice_convert_fusion.7
  200.4 5.6 %multiply_subtract_fusion.1 = f32[4,6,16,16,128]{4,2,1,0,3:T(8,128)} fusion(f32[4,6,16,16,128]{4,2,1,0,3:T(8,128)} %get-tuple-element.203, f32[]{:T(128)S(6)} %mul.2232, f32[4,6,16,16,128]{4,3,2,1,0:T(8,128)} %param.20), kind=kLoop, calls=%fused_computation.560 | loop fusion | flops 1572864 | bytes 9437188 | tf_op jit(solution)/shard_map/sub | solution.py:213
  206.0 2.2 fusion.222
  211.2 1.9 collective-permute-start.5
  214.3 4.9 %collective-permute-start.4 = (f32[4,6,16,128]{3,2,1,0:T(8,128)S(1)}, f32[4,6,16,128]{3,2,1,0:T(8,128)S(1)}, u32[]{:S(2)}, u32[]{:S(2)}) collective-permute-start(f32[4,6,16,128]{3,2,1,0:T(8,128)S(1)} %scatter_fusion.4), channel_id=1, source_target_pairs={{1,0},{2,1},{3,2},{4,3},{5,4},{6,5},{7,6},{8,7},{9,8},{10,9},{11,1... | collective-permute-start | bytes 589832 | tf_op jit(solution)/shard_map/ppermute | solution.py:17
  226.9 1.8 collective-permute-done.6
  230.7 1.3 fusion.183
  232.1 62.9 %while.38 = (s32[]{:T(128)}, f32[4,6,16,16,128]{4,3,2,1,0:T(8,128)}, f32[4,4,6,16,128]{4,3,2,1,0:T(8,128)}, f32[4,6,16,16,128]{4,2,1,0,3:T(8,128)}, bf16[4,10,16...) while((s32[]{:T(128)}, ...), condition=%wide.region_64.65_spmd.clone, body=%wide.region_47.64_spmd.sunk.clone.sunk | while | flops 34659460 | bytes 94720736 | solution.py:205
  236.5 1.4 dynamic-slice_convert_fusion.8
  252.2 1.4 dynamic-slice_convert_fusion.8
  268.0 1.4 dynamic-slice_convert_fusion.8
  283.7 1.4 dynamic-slice_convert_fusion.8
  295.0 5.0 %multiply_subtract_fusion = f32[4,6,16,16,128]{4,3,2,1,0:T(8,128)} fusion(f32[4,6,16,16,128]{4,3,2,1,0:T(8,128)} %param.20, f32[4,6,16,16,128]{4,3,2,1,0:T(8,128)} %get-tuple-element.201, f32[]{:T(128)S(6)} %mul.2230), kind=kLoop, calls=%fused_computation.559 | loop fusion | flops 1572864 | bytes 9437188 | tf_op jit(solution)/shard_map/sub | solution.py:215
  (664 shorter events, 166.7 us)
Async XLA Ops:
  2.6 129.7 %copy-start.16 = (pred[4,4]{1,0:T(4,128)(4,1)}, pred[4,4]{1,0:T(4,128)(4,1)S(1)}, u32[]{:S(2)}) copy-start(pred[4,4]{1,0:T(4,128)(4,1)S(1)} %get-tuple-element.353) | copy-start | bytes 52
  2.6 129.7 %copy-start.21 = (pred[4,4]{1,0:T(4,128)(4,1)}, pred[4,4]{1,0:T(4,128)(4,1)S(1)}, u32[]{:S(2)}) copy-start(pred[4,4]{1,0:T(4,128)(4,1)S(1)} %get-tuple-element.490) | copy-start | bytes 52
  2.6 129.7 %copy-start.23 = (pred[4,4]{1,0:T(4,128)(4,1)}, pred[4,4]{1,0:T(4,128)(4,1)S(1)}, u32[]{:S(2)}) copy-start(pred[4,4]{1,0:T(4,128)(4,1)S(1)} %get-tuple-element.491) | copy-start | bytes 52
  10.0 14.4 %copy-start.33 = (s32[16]{0:T(128)}, s32[16]{0:T(128)S(1)}, u32[]{:S(2)}) copy-start(s32[16]{0:T(128)S(1)} %get-tuple-element.356) | copy-start | bytes 196
  10.3 3.9 %copy-start.29 = (s32[16]{0:T(128)}, s32[16]{0:T(128)S(1)}, u32[]{:S(2)}) copy-start(s32[16]{0:T(128)S(1)} %get-tuple-element.496) | copy-start | bytes 196
  11.5 116.9 %collective-permute-start = (f32[4,6,16,128]{3,2,1,0:T(8,128)S(1)}, f32[4,6,16,128]{3,2,1,0:T(8,128)}, u32[]{:S(2)}, u32[]{:S(2)}) collective-permute-start(f32[4,6,16,128]{3,2,1,0:T(8,128)S(1)} %scatter_fusion), channel_id=1, source_target_pairs={{1,0},{2,1},{3,2},{4,3},{5,4},{6,5},{7,6},{8,7},{9,8},{10,9},{11,1... | collective-permute-start | bytes 589832 | tf_op jit(solution)/shard_map/ppermute | solution.py:17
  17.4 112.7 %collective-permute-start.1 = (f32[4,6,16,128]{3,2,1,0:T(8,128)}, f32[4,6,16,128]{3,2,1,0:T(8,128)}, u32[]{:S(2)}, u32[]{:S(2)}) collective-permute-start(f32[4,6,16,128]{3,2,1,0:T(8,128)} %scatter_fusion.1), channel_id=1, source_target_pairs={{0,1},{1,2},{2,3},{3,4},{4,5},{5,6},{6,7},{7,8},{8,9},{9,10},{10,1... | collective-permute-start | bytes 589832 | tf_op jit(solution)/shard_map/ppermute | solution.py:17
  19.7 4.6 %copy-start.31 = (s32[16]{0:T(128)}, s32[16]{0:T(128)S(1)}, u32[]{:S(2)}) copy-start(s32[16]{0:T(128)S(1)} %fusion.196) | copy-start | bytes 196
  20.9 8.1 %copy-start.41 = (s32[4,4]{1,0:T(4,128)S(1)}, s32[4,4]{1,0:T(4,128)}, u32[]{:S(2)}) copy-start(s32[4,4]{1,0:T(4,128)} %param.24) | copy-start | bytes 196
  20.9 110.8 %collective-permute-start.3 = (f32[1,6,16,128]{3,2,1,0:T(8,128)S(1)}, f32[1,6,16,128]{3,2,1,0:T(8,128)S(1)}, u32[]{:S(2)}, u32[]{:S(2)}) collective-permute-start(f32[1,6,16,128]{3,2,1,0:T(8,128)S(1)} %bitcast.1031), channel_id=1, source_target_pairs={{0,16},{16,32},{32,48},{48,64},{64,80},{80,96},{96,112},{112,128},... | collective-permute-start | bytes 147464 | tf_op jit(solution)/shard_map/ppermute | solution.py:17
  25.5 106.2 %collective-permute-start.2 = (f32[1,6,16,128]{3,2,1,0:T(8,128)S(1)}, f32[1,6,16,128]{3,2,1,0:T(8,128)S(1)}, u32[]{:S(2)}, u32[]{:S(2)}) collective-permute-start(f32[1,6,16,128]{3,2,1,0:T(8,128)S(1)} %bitcast.1032), channel_id=1, source_target_pairs={{16,0},{32,16},{48,32},{64,48},{80,64},{96,80},{112,96},{128,112},... | collective-permute-start | bytes 147464 | tf_op jit(solution)/shard_map/ppermute | solution.py:17
  29.0 103.4 %copy-start.25 = (pred[4,4]{1,0:T(4,128)(4,1)}, pred[4,4]{1,0:T(4,128)(4,1)S(1)}, u32[]{:S(2)}) copy-start(pred[4,4]{1,0:T(4,128)(4,1)S(1)} %broadcast_compare_fusion.3) | copy-start | bytes 52
  32.5 1.9 copy-start.42
  39.1 1.9 copy-start.42
  45.8 1.9 copy-start.42
  57.5 72.5 %copy-start.18 = (s32[1024]{0:T(1024)}, s32[1024]{0:T(1024)S(1)}, u32[]{:S(2)}) copy-start(s32[1024]{0:T(1024)S(1)} %pad_clamp_fusion.2) | copy-start | bytes 12292
  84.4 45.7 %copy-start.19 = (s32[1024]{0:T(1024)}, s32[1024]{0:T(1024)S(1)}, u32[]{:S(2)}) copy-start(s32[1024]{0:T(1024)S(1)} %pad_clamp_fusion.1) | copy-start | bytes 12292
  85.0 45.0 %copy-start.20 = (s32[1024]{0:T(1024)}, s32[1024]{0:T(1024)S(1)}, u32[]{:S(2)}) copy-start(s32[1024]{0:T(1024)S(1)} %pad_clamp_fusion) | copy-start | bytes 12292
  128.5 3.2 %copy-start.35 = (pred[4,4]{1,0:T(4,128)(4,1)S(1)}, pred[4,4]{1,0:T(4,128)(4,1)}, u32[]{:S(2)}) copy-start(pred[4,4]{1,0:T(4,128)(4,1)} %get-tuple-element.349) | copy-start | bytes 52
  128.5 3.2 %copy-start.37 = (pred[4,4]{1,0:T(4,128)(4,1)S(1)}, pred[4,4]{1,0:T(4,128)(4,1)}, u32[]{:S(2)}) copy-start(pred[4,4]{1,0:T(4,128)(4,1)} %get-tuple-element.354) | copy-start | bytes 52
  128.5 3.2 %copy-start.39 = (pred[4,4]{1,0:T(4,128)(4,1)S(1)}, pred[4,4]{1,0:T(4,128)(4,1)}, u32[]{:S(2)}) copy-start(pred[4,4]{1,0:T(4,128)(4,1)} %get-tuple-element.492) | copy-start | bytes 52
  128.5 3.2 %copy-start.40 = (pred[4,4]{1,0:T(4,128)(4,1)S(1)}, pred[4,4]{1,0:T(4,128)(4,1)}, u32[]{:S(2)}) copy-start(pred[4,4]{1,0:T(4,128)(4,1)} %and_and_fusion.2) | copy-start | bytes 52
  209.2 2.0 copy-start.10
  210.1 3.1 %copy-start.28 = (s32[16]{0:T(128)S(1)}, s32[16]{0:T(128)}, u32[]{:S(2)}) copy-start(s32[16]{0:T(128)} %copy-done.27) | copy-start | bytes 196
  211.2 8.0 %copy-start.32 = (s32[16]{0:T(128)S(1)}, s32[16]{0:T(128)}, u32[]{:S(2)}) copy-start(s32[16]{0:T(128)} %copy-done.31) | copy-start | bytes 196
  211.2 14.2 %collective-permute-start.5 = (f32[4,6,16,128]{3,2,1,0:T(8,128)S(1)}, f32[4,6,16,128]{3,2,1,0:T(8,128)S(1)}, u32[]{:S(2)}, u32[]{:S(2)}) collective-permute-start(f32[4,6,16,128]{3,2,1,0:T(8,128)S(1)} %scatter_fusion.5), channel_id=1, source_target_pairs={{0,1},{1,2},{2,3},{3,4},{4,5},{5,6},{6,7},{7,8},{8,9},{9,10},{10,1... | collective-permute-start | bytes 589832 | tf_op jit(solution)/shard_map/ppermute | solution.py:17
  214.3 7.3 %copy-start.34 = (s32[16]{0:T(128)S(1)}, s32[16]{0:T(128)}, u32[]{:S(2)}) copy-start(s32[16]{0:T(128)} %copy-done.33) | copy-start | bytes 196
  214.3 11.8 %collective-permute-start.4 = (f32[4,6,16,128]{3,2,1,0:T(8,128)S(1)}, f32[4,6,16,128]{3,2,1,0:T(8,128)S(1)}, u32[]{:S(2)}, u32[]{:S(2)}) collective-permute-start(f32[4,6,16,128]{3,2,1,0:T(8,128)S(1)} %scatter_fusion.4), channel_id=1, source_target_pairs={{1,0},{2,1},{3,2},{4,3},{5,4},{6,5},{7,6},{8,7},{9,8},{10,9},{11,1... | collective-permute-start | bytes 589832 | tf_op jit(solution)/shard_map/ppermute | solution.py:17
  220.3 6.6 %collective-permute-start.7 = (f32[1,6,16,128]{3,2,1,0:T(8,128)S(1)}, f32[1,6,16,128]{3,2,1,0:T(8,128)S(1)}, u32[]{:S(2)}, u32[]{:S(2)}) collective-permute-start(f32[1,6,16,128]{3,2,1,0:T(8,128)S(1)} %bitcast.1030), channel_id=1, source_target_pairs={{0,16},{16,32},{32,48},{48,64},{64,80},{80,96},{96,112},{112,128},... | collective-permute-start | bytes 147464 | tf_op jit(solution)/shard_map/ppermute | solution.py:17
  222.7 6.0 %collective-permute-start.6 = (f32[1,6,16,128]{3,2,1,0:T(8,128)S(1)}, f32[1,6,16,128]{3,2,1,0:T(8,128)S(1)}, u32[]{:S(2)}, u32[]{:S(2)}) collective-permute-start(f32[1,6,16,128]{3,2,1,0:T(8,128)S(1)} %bitcast.1029), channel_id=1, source_target_pairs={{16,0},{32,16},{48,32},{64,48},{80,64},{96,80},{112,96},{128,112},... | collective-permute-start | bytes 147464 | tf_op jit(solution)/shard_map/ppermute | solution.py:17
  225.4 3.3 %copy-start.36 = (pred[4,4]{1,0:T(4,128)(4,1)S(1)}, pred[4,4]{1,0:T(4,128)(4,1)}, u32[]{:S(2)}) copy-start(pred[4,4]{1,0:T(4,128)(4,1)} %get-tuple-element.349) | copy-start | bytes 52
  225.4 3.3 %copy-start.38 = (pred[4,4]{1,0:T(4,128)(4,1)S(1)}, pred[4,4]{1,0:T(4,128)(4,1)}, u32[]{:S(2)}) copy-start(pred[4,4]{1,0:T(4,128)(4,1)} %get-tuple-element.354) | copy-start | bytes 52
  (26 other events, 26.2 us)

commit v2 on v1

--- a/solution.py
+++ b/solution.py
@@ -208,7 +208,8 @@
         )
 
     limits = lax.map(lambda operands: time_limit(operands[0], operands[1]), (state, metrics))
-    step = CFL_NUMBER * lax.pmin(lax.pmin(jnp.min(limits), "gy"), "gx")
+    gathered = lax.all_gather(jnp.broadcast_to(jnp.min(limits), (1024,)), ("gx", "gy"), tiled=True)
+    step = CFL_NUMBER * jnp.min(gathered)
     first = residual_local(state)
     middle = state - 0.5 * step * first
     second = residual_local(middle)

time: 303 us -> 281 us (0.927)
  the two profiles are of different devices: /device:TPU:128 before, /device:TPU:40 now
where the time goes in v2:
time: 281 us; the launch traced here: 279 us
  other arithmetic  140 us (50%)
  local copies, waits for them, and re-layouts  68 us (24%)
  starting transfers between devices  25.8 us (9%)
  waiting for transfers between devices  25.5 us (9%)
  between operations  16.2 us (6%)
    ppermute x8, starting transfers between devices, shifted(): lax.ppermute(value, axis, [(source, source + steps) for source in range(i...  25.8 us
    all_gather x1, waiting for transfers between devices, per_device(): lax.all_gather(jnp.broadcast_to(jnp.min(limits), (1024,)), ('gx', 'gy'),...  25.5 us
    reduce_sum x28, other arithmetic, euler_flux(): normal = jnp.sum(velocity * area, axis=0)  16.6 us
    sub x24, other arithmetic, flux_balance(): flux = flux - viscous  13.4 us
    convert_element_type x8, other arithmetic, block_residual(): geometry = metric.astype(jnp.float32)  10.9 us
    scatter x8, local copies, waits for them, and re-layouts, pack(): outgoing.at[jnp.where(sending, send_slot, capacity)].set(flat, mode='drop')  10.9 us
    mul x24, other arithmetic, flux_balance(): 0.5 * jnp.maximum(speed_left, speed_right) * jump  9.22 us
    add x24, other arithmetic, euler_flux(): cons[1:4] * normal + pressure * area  7.44 us
  transfers between devices with their start and end apart: 9, of which 1 were waited for; matrix products, arithmetic and copies ran while one was open for 41% of the time, Pallas kernels for 0%

profile of v2, /device:TPU:40, one launch (start us, length us, event | category | flops | bytes accessed | tf_op | source)
XLA Modules:
  0.0 278.7 jit_solution(16695476215873168438)
XLA Ops:
  11.8 2.9 %copy.132 = f32[4,6,16,16,128]{4,2,1,0,3:T(8,128)S(1)} copy(f32[4,6,16,16,128]{4,3,2,1,0:T(8,128)} %param.20) | data formatting | bytes 6291456 | tf_op args[0]
  18.8 1.9 collective-permute-start
  21.4 3.2 %scatter_fusion.1 = f32[4,6,16,128]{3,2,1,0:T(8,128)} fusion(f32[4,6,16,128]{3,2,1,0:T(8,128)} %broadcast.2355.clone.2, s32[16]{0:T(128)S(1)} %get-tuple-element.501, f32[16,6,16,128]{3,2,1,0:T(8,128)S(1)} %bitcast.1020), kind=kCustom, calls=%fused_computation.7 | custom fusion | bytes 2359360 | tf_op jit(solution)/shard_map/scatter | solution.py:182
  24.6 2.4 collective-permute-start.1
  28.2 3.4 %collective-permute-start.3 = (f32[1,6,16,128]{3,2,1,0:T(8,128)S(1)}, f32[1,6,16,128]{3,2,1,0:T(8,128)S(1)}, u32[]{:S(2)}, u32[]{:S(2)}) collective-permute-start(f32[1,6,16,128]{3,2,1,0:T(8,128)S(1)} %bitcast.1031), channel_id=1, source_target_pairs={{0,16},{16,32},{32,48},{48,64},{64,80},{80,96},{96,112},{112,128},... | collective-permute-start | bytes 147464 | tf_op jit(solution)/shard_map/ppermute | solution.py:17
  32.7 4.6 %collective-permute-start.2 = (f32[1,6,16,128]{3,2,1,0:T(8,128)S(1)}, f32[1,6,16,128]{3,2,1,0:T(8,128)S(1)}, u32[]{:S(2)}, u32[]{:S(2)}) collective-permute-start(f32[1,6,16,128]{3,2,1,0:T(8,128)S(1)} %bitcast.1032), channel_id=1, source_target_pairs={{16,0},{32,16},{48,32},{64,48},{80,64},{96,80},{112,96},{128,112},... | collective-permute-start | bytes 147464 | tf_op jit(solution)/shard_map/ppermute | solution.py:17
  37.3 26.2 %while.36 = (s32[]{:T(128)}, f32[4]{0:T(128)}, bf16[4,10,16,16,128]{4,3,2,1,0:T(8,128)(2,1)}, f32[4,6,16,16,128]{4,3,2,1,0:T(8,128)}, s32[]{:T(128)}, /*index=5*/s32[]{:T(128)}, s32[]{}, s32[]{}) while((s32[]{:T(128)}, f32[4]{0:T(128)}, bf16[4,10,16,16,128]{4,3,2,1,0:T(8,128)(2,1)}, f32[4,6,16,16,128]{4,3,2,1,0:T(8,128)}, s32[]{:T(128)}, ...), condition=%wide.region_9.10_spmd, body=%wide.region_0.9_spmd.sunk | while | flops 2195459 | bytes 6160717 | solution.py:210
  40.8 1.9 fusion.273
  47.3 1.9 fusion.273
  53.9 1.9 fusion.273
  60.4 1.9 fusion.273
  70.2 1.5 gather_fusion
  71.7 2.4 gather_fusion.1
  74.2 1.4 select_select_fusion.1
  78.2 66.0 %while.37 = (s32[]{:T(128)}, f32[4,6,16,16,128]{4,2,1,0,3:T(8,128)}, f32[4,4,6,16,128]{4,3,2,1,0:T(8,128)}, f32[4,6,16,16,128]{4,3,2,1,0:T(8,128)}, bf16[4,10,16...) while((s32[]{:T(128)}, ...), condition=%wide.region_41.42_spmd.clone, body=%wide.region_24.41_spmd.sunk.clone.sunk | while | flops 34659460 | bytes 94720760 | solution.py:205
  82.1 1.4 dynamic-slice_convert_fusion.7
  98.6 1.4 dynamic-slice_convert_fusion.7
  115.1 1.4 dynamic-slice_convert_fusion.7
  131.6 1.4 dynamic-slice_convert_fusion.7
  144.2 25.5 %all-gather.2.cloned.1.call-done = f32[262144]{0:T(1024)} async-done(((f32[1024]{0:T(1024)}), f32[262144]{0:T(1024)}) %all-gather.2.cloned.1.call-update) | async-done | bytes 1048592 | tf_op jit(solution)/shard_map/all_gather | solution.py:211
  169.7 2.1 reduce_min.28
  172.4 3.9 %multiply_subtract_fusion.1 = f32[4,6,16,16,128]{4,2,1,0,3:T(8,128)S(1)} fusion(f32[4,6,16,16,128]{4,2,1,0,3:T(8,128)} %get-tuple-element.203, f32[]{:T(128)S(6)} %mul.2232, f32[4,6,16,16,128]{4,3,2,1,0:T(8,128)} %param.20), kind=kLoop, calls=%fused_computation.560 | loop fusion | flops 1572864 | bytes 9437188 | tf_op jit(solution)/shard_map/sub | solution.py:214
  179.3 2.1 collective-permute-start.5
  182.6 3.4 %collective-permute-start.4 = (f32[4,6,16,128]{3,2,1,0:T(8,128)S(1)}, f32[4,6,16,128]{3,2,1,0:T(8,128)S(1)}, u32[]{:S(2)}, u32[]{:S(2)}) collective-permute-start(f32[4,6,16,128]{3,2,1,0:T(8,128)S(1)} %scatter_fusion.4), channel_id=1, source_target_pairs={{1,0},{2,1},{3,2},{4,3},{5,4},{6,5},{7,6},{8,7},{9,8},{10,9},{11,1... | collective-permute-start | bytes 589832 | tf_op jit(solution)/shard_map/ppermute | solution.py:17
  187.1 3.4 %collective-permute-start.7 = (f32[1,6,16,128]{3,2,1,0:T(8,128)S(1)}, f32[1,6,16,128]{3,2,1,0:T(8,128)S(1)}, u32[]{:S(2)}, u32[]{:S(2)}) collective-permute-start(f32[1,6,16,128]{3,2,1,0:T(8,128)S(1)} %bitcast.1030), channel_id=1, source_target_pairs={{0,16},{16,32},{32,48},{48,64},{64,80},{80,96},{96,112},{112,128},... | collective-permute-start | bytes 147464 | tf_op jit(solution)/shard_map/ppermute | solution.py:17
  191.7 4.6 %collective-permute-start.6 = (f32[1,6,16,128]{3,2,1,0:T(8,128)S(1)}, f32[1,6,16,128]{3,2,1,0:T(8,128)S(1)}, u32[]{:S(2)}, u32[]{:S(2)}) collective-permute-start(f32[1,6,16,128]{3,2,1,0:T(8,128)S(1)} %bitcast.1029), channel_id=1, source_target_pairs={{16,0},{32,16},{48,32},{64,48},{80,64},{96,80},{112,96},{128,112},... | collective-permute-start | bytes 147464 | tf_op jit(solution)/shard_map/ppermute | solution.py:17
  198.4 1.6 gather_fusion.3
  200.0 1.4 select_select_fusion
  203.9 62.9 %while.38 = (s32[]{:T(128)}, f32[4,6,16,16,128]{4,3,2,1,0:T(8,128)}, f32[4,4,6,16,128]{4,3,2,1,0:T(8,128)}, f32[4,6,16,16,128]{4,2,1,0,3:T(8,128)}, bf16[4,10,16...) while((s32[]{:T(128)}, ...), condition=%wide.region_63.64_spmd.clone, body=%wide.region_46.63_spmd.sunk.clone.sunk | while | flops 34659460 | bytes 94720736 | solution.py:205
  208.3 1.4 dynamic-slice_convert_fusion.8
  224.1 1.4 dynamic-slice_convert_fusion.8
  266.8 5.0 %multiply_subtract_fusion = f32[4,6,16,16,128]{4,3,2,1,0:T(8,128)} fusion(f32[4,6,16,16,128]{4,3,2,1,0:T(8,128)} %param.20, f32[4,6,16,16,128]{4,3,2,1,0:T(8,128)} %get-tuple-element.201, f32[]{:T(128)S(6)} %mul.2230), kind=kLoop, calls=%fused_computation.559 | loop fusion | flops 1572864 | bytes 9437188 | tf_op jit(solution)/shard_map/sub | solution.py:216
  (671 shorter events, 167.4 us)
Async XLA Ops:
  7.2 162.5 %all-gather.2.cloned.1.call-start = ((), (), s32[]{:S(2)}) async-start(), calls=%async_computation | async-start | bytes 1052672 | tf_op jit(solution)/shard_map/all_gather | solution.py:211
  9.3 66.6 %copy-start.17 = (pred[4,4]{1,0:T(4,128)(4,1)}, pred[4,4]{1,0:T(4,128)(4,1)S(1)}, u32[]{:S(2)}) copy-start(pred[4,4]{1,0:T(4,128)(4,1)S(1)} %get-tuple-element.358) | copy-start | bytes 52
  9.3 66.7 %copy-start.22 = (pred[4,4]{1,0:T(4,128)(4,1)}, pred[4,4]{1,0:T(4,128)(4,1)S(1)}, u32[]{:S(2)}) copy-start(pred[4,4]{1,0:T(4,128)(4,1)S(1)} %get-tuple-element.495) | copy-start | bytes 52
  16.0 2.8 copy-start.7
  16.0 2.8 copy-start.9
  16.7 14.9 %copy-start.34 = (s32[16]{0:T(128)}, s32[16]{0:T(128)S(1)}, u32[]{:S(2)}) copy-start(s32[16]{0:T(128)S(1)} %get-tuple-element.361) | copy-start | bytes 196
  17.5 3.9 %copy-start.28 = (s32[16]{0:T(128)}, s32[16]{0:T(128)S(1)}, u32[]{:S(2)}) copy-start(s32[16]{0:T(128)S(1)} %get-tuple-element.501) | copy-start | bytes 196
  18.8 51.4 %collective-permute-start = (f32[4,6,16,128]{3,2,1,0:T(8,128)S(1)}, f32[4,6,16,128]{3,2,1,0:T(8,128)}, u32[]{:S(2)}, u32[]{:S(2)}) collective-permute-start(f32[4,6,16,128]{3,2,1,0:T(8,128)S(1)} %scatter_fusion), channel_id=1, source_target_pairs={{1,0},{2,1},{3,2},{4,3},{5,4},{6,5},{7,6},{8,7},{9,8},{10,9},{11,1... | collective-permute-start | bytes 589832 | tf_op jit(solution)/shard_map/ppermute | solution.py:17
  24.6 47.1 %collective-permute-start.1 = (f32[4,6,16,128]{3,2,1,0:T(8,128)}, f32[4,6,16,128]{3,2,1,0:T(8,128)}, u32[]{:S(2)}, u32[]{:S(2)}) collective-permute-start(f32[4,6,16,128]{3,2,1,0:T(8,128)} %scatter_fusion.1), channel_id=1, source_target_pairs={{0,1},{1,2},{2,3},{3,4},{4,5},{5,6},{6,7},{7,8},{8,9},{9,10},{10,1... | collective-permute-start | bytes 589832 | tf_op jit(solution)/shard_map/ppermute | solution.py:17
  27.1 4.5 %copy-start.30 = (s32[16]{0:T(128)}, s32[16]{0:T(128)S(1)}, u32[]{:S(2)}) copy-start(s32[16]{0:T(128)S(1)} %fusion.196) | copy-start | bytes 196
  28.2 46.0 %collective-permute-start.3 = (f32[1,6,16,128]{3,2,1,0:T(8,128)S(1)}, f32[1,6,16,128]{3,2,1,0:T(8,128)S(1)}, u32[]{:S(2)}, u32[]{:S(2)}) collective-permute-start(f32[1,6,16,128]{3,2,1,0:T(8,128)S(1)} %bitcast.1031), channel_id=1, source_target_pairs={{0,16},{16,32},{32,48},{48,64},{64,80},{80,96},{96,112},{112,128},... | collective-permute-start | bytes 147464 | tf_op jit(solution)/shard_map/ppermute | solution.py:17
  32.7 41.4 %collective-permute-start.2 = (f32[1,6,16,128]{3,2,1,0:T(8,128)S(1)}, f32[1,6,16,128]{3,2,1,0:T(8,128)S(1)}, u32[]{:S(2)}, u32[]{:S(2)}) collective-permute-start(f32[1,6,16,128]{3,2,1,0:T(8,128)S(1)} %bitcast.1032), channel_id=1, source_target_pairs={{16,0},{32,16},{48,32},{64,48},{80,64},{96,80},{112,96},{128,112},... | collective-permute-start | bytes 147464 | tf_op jit(solution)/shard_map/ppermute | solution.py:17
  66.8 4.9 %copy-start.19 = (s32[1024]{0:T(1024)}, s32[1024]{0:T(1024)S(1)}, u32[]{:S(2)}) copy-start(s32[1024]{0:T(1024)S(1)} %pad_clamp_fusion.2) | copy-start | bytes 12292
  68.1 6.0 %copy-start.38 = (pred[4,4]{1,0:T(4,128)(4,1)}, pred[4,4]{1,0:T(4,128)(4,1)S(1)}, u32[]{:S(2)}) copy-start(pred[4,4]{1,0:T(4,128)(4,1)S(1)} %get-tuple-element.359) | copy-start | bytes 52
  68.1 6.0 %copy-start.40 = (pred[4,4]{1,0:T(4,128)(4,1)}, pred[4,4]{1,0:T(4,128)(4,1)S(1)}, u32[]{:S(2)}) copy-start(pred[4,4]{1,0:T(4,128)(4,1)S(1)} %get-tuple-element.497) | copy-start | bytes 52
  68.1 6.0 %copy-start.42 = (pred[4,4]{1,0:T(4,128)(4,1)}, pred[4,4]{1,0:T(4,128)(4,1)S(1)}, u32[]{:S(2)}) copy-start(pred[4,4]{1,0:T(4,128)(4,1)S(1)} %and_and_fusion.2) | copy-start | bytes 52
  68.8 7.1 %copy-start.32 = (pred[4,4]{1,0:T(4,128)(4,1)}, pred[4,4]{1,0:T(4,128)(4,1)S(1)}, u32[]{:S(2)}) copy-start(pred[4,4]{1,0:T(4,128)(4,1)S(1)} %broadcast_compare_fusion.3) | copy-start | bytes 52
  68.9 2.9 %copy-start.20 = (s32[1024]{0:T(1024)}, s32[1024]{0:T(1024)S(1)}, u32[]{:S(2)}) copy-start(s32[1024]{0:T(1024)S(1)} %pad_clamp_fusion.1) | copy-start | bytes 12292
  69.5 2.2 copy-start.21
  70.1 4.0 %copy-start.36 = (pred[4,4]{1,0:T(4,128)(4,1)S(1)}, pred[4,4]{1,0:T(4,128)(4,1)}, u32[]{:S(2)}) copy-start(pred[4,4]{1,0:T(4,128)(4,1)} %get-tuple-element.354) | copy-start | bytes 52
  176.7 2.6 copy-start.11
  178.1 3.3 %copy-start.27 = (s32[16]{0:T(128)S(1)}, s32[16]{0:T(128)}, u32[]{:S(2)}) copy-start(s32[16]{0:T(128)} %copy-done.26) | copy-start | bytes 196
  179.3 6.8 %copy-start.31 = (s32[16]{0:T(128)S(1)}, s32[16]{0:T(128)}, u32[]{:S(2)}) copy-start(s32[16]{0:T(128)} %copy-done.30) | copy-start | bytes 196
  179.3 18.3 %collective-permute-start.5 = (f32[4,6,16,128]{3,2,1,0:T(8,128)S(1)}, f32[4,6,16,128]{3,2,1,0:T(8,128)S(1)}, u32[]{:S(2)}, u32[]{:S(2)}) collective-permute-start(f32[4,6,16,128]{3,2,1,0:T(8,128)S(1)} %scatter_fusion.5), channel_id=1, source_target_pairs={{0,1},{1,2},{2,3},{3,4},{4,5},{5,6},{6,7},{7,8},{8,9},{9,10},{10,1... | collective-permute-start | bytes 589832 | tf_op jit(solution)/shard_map/ppermute | solution.py:17
  182.6 8.0 %copy-start.35 = (s32[16]{0:T(128)S(1)}, s32[16]{0:T(128)}, u32[]{:S(2)}) copy-start(s32[16]{0:T(128)} %copy-done.34) | copy-start | bytes 196
  182.6 15.8 %collective-permute-start.4 = (f32[4,6,16,128]{3,2,1,0:T(8,128)S(1)}, f32[4,6,16,128]{3,2,1,0:T(8,128)S(1)}, u32[]{:S(2)}, u32[]{:S(2)}) collective-permute-start(f32[4,6,16,128]{3,2,1,0:T(8,128)S(1)} %scatter_fusion.4), channel_id=1, source_target_pairs={{1,0},{2,1},{3,2},{4,3},{5,4},{6,5},{7,6},{8,7},{9,8},{10,9},{11,1... | collective-permute-start | bytes 589832 | tf_op jit(solution)/shard_map/ppermute | solution.py:17
  187.1 12.9 %collective-permute-start.7 = (f32[1,6,16,128]{3,2,1,0:T(8,128)S(1)}, f32[1,6,16,128]{3,2,1,0:T(8,128)S(1)}, u32[]{:S(2)}, u32[]{:S(2)}) collective-permute-start(f32[1,6,16,128]{3,2,1,0:T(8,128)S(1)} %bitcast.1030), channel_id=1, source_target_pairs={{0,16},{16,32},{32,48},{48,64},{64,80},{80,96},{96,112},{112,128},... | collective-permute-start | bytes 147464 | tf_op jit(solution)/shard_map/ppermute | solution.py:17
  191.7 8.3 %collective-permute-start.6 = (f32[1,6,16,128]{3,2,1,0:T(8,128)S(1)}, f32[1,6,16,128]{3,2,1,0:T(8,128)S(1)}, u32[]{:S(2)}, u32[]{:S(2)}) collective-permute-start(f32[1,6,16,128]{3,2,1,0:T(8,128)S(1)} %bitcast.1029), channel_id=1, source_target_pairs={{16,0},{32,16},{48,32},{64,48},{80,64},{96,80},{112,96},{128,112},... | collective-permute-start | bytes 147464 | tf_op jit(solution)/shard_map/ppermute | solution.py:17
  197.6 2.4 copy-start.37
  197.6 2.4 copy-start.39
  197.6 2.4 copy-start.41
  197.6 2.4 copy-start.43
  (29 other events, 35.6 us)
Sparse Core Ops, SparseCore 0:
  66.2 103.3 all-gather.1

commit v3 on v2

--- a/solution.py
+++ b/solution.py
@@ -207,7 +207,7 @@
             (cells, halos, metrics),
         )
 
-    limits = lax.map(lambda operands: time_limit(operands[0], operands[1]), (state, metrics))
+    limits = jax.vmap(time_limit)(state, metrics)
     gathered = lax.all_gather(jnp.broadcast_to(jnp.min(limits), (1024,)), ("gx", "gy"), tiled=True)
     step = CFL_NUMBER * jnp.min(gathered)
     first = residual_local(state)

time: 281 us -> 256 us (0.911)
  other arithmetic: 140 us -> 122 us
  local copies, waits for them, and re-layouts: 68 us -> 57.4 us
  waiting for transfers between devices: 25.5 us -> 29.7 us
    reduce_min x4 -> x0, other arithmetic: 7.4 us -> none  [time_limit(): return jnp.min(geometry[9] / total)]
    reduce_sum x28 -> x25, other arithmetic: 16.6 us -> 12.4 us  [euler_flux(): normal = jnp.sum(velocity * area, axis=0)]
    all_gather x1, waiting for transfers between devices: 25.5 us -> 29.6 us  [per_device(): lax.all_gather(jnp.broadcast_to(jnp.min(limits), (1024,)), ('gx', 'gy'),...]
    dynamic_update_slice x4 -> x0, local copies, waits for them, and re-layouts: 2.92 us -> none  [per_device(): lax.map(lambda operands: time_limit(operands[0], operands[1]), (state, me...]
    unnamed x89 -> x73, local copies, waits for them, and re-layouts: 5.89 us -> 5.16 us
  transfers between devices with their start and end apart: 9 -> 9, of which waited for: 1 -> 1; matrix products, arithmetic and copies ran while one was open for 41% -> 35% of each run, Pallas kernels for 0% -> 0%
where the time goes in v3:
time: 256 us; the launch traced here: 254 us
  other arithmetic  122 us (48%)
  local copies, waits for them, and re-layouts  57.4 us (22%)
  waiting for transfers between devices  29.7 us (12%)
  starting transfers between devices  25.8 us (10%)
  between operations  16.3 us (6%)
  loops' own time  2.66 us (1%)
    all_gather x1, waiting for transfers between devices, per_device(): lax.all_gather(jnp.broadcast_to(jnp.min(limits), (1024,)), ('gx', 'gy'),...  29.6 us
    ppermute x8, starting transfers between devices, shifted(): lax.ppermute(value, axis, [(source, source + steps) for source in range(i...  25.8 us
    sub x24, other arithmetic, flux_balance(): flux = flux - viscous  13.4 us
    reduce_sum x25, other arithmetic, euler_flux(): normal = jnp.sum(velocity * area, axis=0)  12.4 us
    convert_element_type x8, other arithmetic, block_residual(): geometry = metric.astype(jnp.float32)  10.9 us
    mul x24, other arithmetic, flux_balance(): 0.5 * jnp.maximum(speed_left, speed_right) * jump  9.22 us
    scatter x8, local copies, waits for them, and re-layouts, pack(): outgoing.at[jnp.where(sending, send_slot, capacity)].set(flat, mode='drop')  8.8 us
    add x24, other arithmetic, euler_flux(): cons[1:4] * normal + pressure * area  7.43 us
  transfers between devices with their start and end apart: 9, of which 1 were waited for; matrix products, arithmetic and copies ran while one was open for 35% of the time, Pallas kernels for 0%

profile of v3, /device:TPU:40, one launch (start us, length us, event | category | flops | bytes accessed | tf_op | source)
XLA Modules:
  0.0 254.0 jit_solution(15103868238616170221)
XLA Ops:
  11.2 2.9 %copy.142 = f32[4,6,16,16,128]{4,2,1,0,3:T(8,128)S(1)} copy(f32[4,6,16,16,128]{4,3,2,1,0:T(8,128)} %param.18) | data formatting | bytes 6291456 | tf_op args[0]
  17.3 1.9 collective-permute-start
  20.4 2.4 collective-permute-start.1
  23.9 3.4 %collective-permute-start.3 = (f32[1,6,16,128]{3,2,1,0:T(8,128)S(1)}, f32[1,6,16,128]{3,2,1,0:T(8,128)S(1)}, u32[]{:S(2)}, u32[]{:S(2)}) collective-permute-start(f32[1,6,16,128]{3,2,1,0:T(8,128)S(1)} %bitcast.986), channel_id=1, source_target_pairs={{0,16},{16,32},{32,48},{48,64},{64,80},{80,96},{96,112},{112,128},... | collective-permute-start | bytes 147464 | tf_op jit(solution)/shard_map/ppermute | solution.py:17
  28.5 4.6 %collective-permute-start.2 = (f32[1,6,16,128]{3,2,1,0:T(8,128)S(1)}, f32[1,6,16,128]{3,2,1,0:T(8,128)S(1)}, u32[]{:S(2)}, u32[]{:S(2)}) collective-permute-start(f32[1,6,16,128]{3,2,1,0:T(8,128)S(1)} %bitcast.987), channel_id=1, source_target_pairs={{16,0},{32,16},{48,32},{64,48},{80,64},{96,80},{112,96},{128,112},... | collective-permute-start | bytes 147464 | tf_op jit(solution)/shard_map/ppermute | solution.py:17
  34.1 2.5 %convert_element_type.45 = f32[4,10,16,16,128]{4,3,2,1,0:T(8,128)S(1)} convert(bf16[4,10,16,16,128]{4,3,2,1,0:T(8,128)(2,1)} %param.19) | non-fusion elementwise | flops 1310720 | bytes 7864320 | tf_op jit(solution)/shard_map/vmap()/convert_element_type | solution.py:127
  37.9 1.4 fusion.183
  41.4 1.5 gather_fusion
  42.9 1.5 gather_fusion.1
  44.5 1.6 select_select_fusion.1
  47.1 1.3 fusion.176
  48.5 66.0 %while.26 = (s32[]{:T(128)}, f32[4,6,16,16,128]{4,2,1,0,3:T(8,128)}, f32[4,4,6,16,128]{4,3,2,1,0:T(8,128)}, f32[4,6,16,16,128]{4,3,2,1,0:T(8,128)}, bf16[4,10,16...) while((s32[]{:T(128)}, ...), condition=%wide.region_38.39_spmd.clone, body=%wide.region_21.38_spmd.sunk.clone.sunk | while | flops 34659460 | bytes 94720760 | solution.py:205
  52.5 1.4 dynamic-slice_convert_fusion.4
  69.0 1.4 dynamic-slice_convert_fusion.4
  85.5 1.4 dynamic-slice_convert_fusion.4
  102.0 1.4 dynamic-slice_convert_fusion.4
  114.5 29.6 %all-gather.2.cloned.1.call-done = f32[262144]{0:T(1024)} async-done(((f32[1024]{0:T(1024)}), f32[262144]{0:T(1024)}) %all-gather.2.cloned.1.call-update) | async-done | bytes 1048592 | tf_op jit(solution)/shard_map/all_gather | solution.py:211
  144.1 2.2 reduce_min.20
  147.0 3.9 %multiply_subtract_fusion.1 = f32[4,6,16,16,128]{4,2,1,0,3:T(8,128)S(1)} fusion(f32[4,6,16,16,128]{4,2,1,0,3:T(8,128)} %get-tuple-element.180, f32[]{:T(128)S(6)} %mul.2245, f32[4,6,16,16,128]{4,3,2,1,0:T(8,128)} %get-tuple-element.933), kind=kLoop, calls=%fused_computation.536 | loop fusion | flops 1572864 | bytes 9437188 | tf_op jit(solution)/shard_map/sub | solution.py:214
  153.8 2.1 collective-permute-start.5
  157.1 3.4 %collective-permute-start.4 = (f32[4,6,16,128]{3,2,1,0:T(8,128)S(1)}, f32[4,6,16,128]{3,2,1,0:T(8,128)S(1)}, u32[]{:S(2)}, u32[]{:S(2)}) collective-permute-start(f32[4,6,16,128]{3,2,1,0:T(8,128)S(1)} %scatter_fusion.4), channel_id=1, source_target_pairs={{1,0},{2,1},{3,2},{4,3},{5,4},{6,5},{7,6},{8,7},{9,8},{10,9},{11,1... | collective-permute-start | bytes 589832 | tf_op jit(solution)/shard_map/ppermute | solution.py:17
  161.6 3.4 %collective-permute-start.7 = (f32[1,6,16,128]{3,2,1,0:T(8,128)S(1)}, f32[1,6,16,128]{3,2,1,0:T(8,128)S(1)}, u32[]{:S(2)}, u32[]{:S(2)}) collective-permute-start(f32[1,6,16,128]{3,2,1,0:T(8,128)S(1)} %bitcast.985), channel_id=1, source_target_pairs={{0,16},{16,32},{32,48},{48,64},{64,80},{80,96},{96,112},{112,128},... | collective-permute-start | bytes 147464 | tf_op jit(solution)/shard_map/ppermute | solution.py:17
  166.1 4.6 %collective-permute-start.6 = (f32[1,6,16,128]{3,2,1,0:T(8,128)S(1)}, f32[1,6,16,128]{3,2,1,0:T(8,128)S(1)}, u32[]{:S(2)}, u32[]{:S(2)}) collective-permute-start(f32[1,6,16,128]{3,2,1,0:T(8,128)S(1)} %bitcast.984), channel_id=1, source_target_pairs={{16,0},{32,16},{48,32},{64,48},{80,64},{96,80},{112,96},{128,112},... | collective-permute-start | bytes 147464 | tf_op jit(solution)/shard_map/ppermute | solution.py:17
  172.2 1.6 gather_fusion.4
  173.8 1.6 gather_fusion.3
  175.5 1.6 select_select_fusion
  179.1 63.0 %while.27 = (s32[]{:T(128)}, f32[4,6,16,16,128]{4,3,2,1,0:T(8,128)}, f32[4,4,6,16,128]{4,3,2,1,0:T(8,128)}, f32[4,6,16,16,128]{4,2,1,0,3:T(8,128)}, bf16[4,10,16...) while((s32[]{:T(128)}, ...), condition=%wide.region_60.61_spmd.clone, body=%wide.region_43.60_spmd.sunk.clone.sunk | while | flops 34659460 | bytes 94720736 | solution.py:205
  183.6 1.4 dynamic-slice_convert_fusion.5
  199.3 1.4 dynamic-slice_convert_fusion.5
  215.0 1.4 dynamic-slice_convert_fusion.5
  230.8 1.4 dynamic-slice_convert_fusion.5
  242.1 5.0 %multiply_subtract_fusion = f32[4,6,16,16,128]{4,3,2,1,0:T(8,128)} fusion(f32[4,6,16,16,128]{4,3,2,1,0:T(8,128)} %get-tuple-element.933, f32[4,6,16,16,128]{4,3,2,1,0:T(8,128)} %get-tuple-element.179, f32[]{:T(128)S(6)} %mul.2243), kind=kLoop, calls=%fused_computation.535 | loop fusion | flops 1572864 | bytes 9437188 | tf_op jit(solution)/shard_map/sub | solution.py:216
  (620 shorter events, 139.8 us)
Async XLA Ops:
  7.2 137.0 %all-gather.2.cloned.1.call-start = ((), (), s32[]{:S(2)}) async-start(), calls=%async_computation | async-start | bytes 1052672 | tf_op jit(solution)/shard_map/all_gather | solution.py:211
  8.7 35.7 %copy-start.27 = (pred[4,4]{1,0:T(4,128)(4,1)}, pred[4,4]{1,0:T(4,128)(4,1)S(1)}, u32[]{:S(2)}) copy-start(pred[4,4]{1,0:T(4,128)(4,1)S(1)} %get-tuple-element.323) | copy-start | bytes 52
  8.7 37.9 %copy-start.8 = (pred[4,4]{1,0:T(4,128)(4,1)}, pred[4,4]{1,0:T(4,128)(4,1)S(1)}, u32[]{:S(2)}) copy-start(pred[4,4]{1,0:T(4,128)(4,1)S(1)} %get-tuple-element.327) | copy-start | bytes 52
  8.7 37.9 %copy-start.13 = (pred[4,4]{1,0:T(4,128)(4,1)}, pred[4,4]{1,0:T(4,128)(4,1)S(1)}, u32[]{:S(2)}) copy-start(pred[4,4]{1,0:T(4,128)(4,1)S(1)} %get-tuple-element.464) | copy-start | bytes 52
  8.7 37.9 %copy-start.15 = (pred[4,4]{1,0:T(4,128)(4,1)}, pred[4,4]{1,0:T(4,128)(4,1)S(1)}, u32[]{:S(2)}) copy-start(pred[4,4]{1,0:T(4,128)(4,1)S(1)} %get-tuple-element.465) | copy-start | bytes 52
  15.5 11.8 %copy-start.25 = (s32[16]{0:T(128)}, s32[16]{0:T(128)S(1)}, u32[]{:S(2)}) copy-start(s32[16]{0:T(128)S(1)} %get-tuple-element.330) | copy-start | bytes 196
  15.8 3.4 %copy-start.19 = (s32[16]{0:T(128)}, s32[16]{0:T(128)S(1)}, u32[]{:S(2)}) copy-start(s32[16]{0:T(128)S(1)} %get-tuple-element.470) | copy-start | bytes 196
  17.3 24.1 %collective-permute-start = (f32[4,6,16,128]{3,2,1,0:T(8,128)S(1)}, f32[4,6,16,128]{3,2,1,0:T(8,128)S(1)}, u32[]{:S(2)}, u32[]{:S(2)}) collective-permute-start(f32[4,6,16,128]{3,2,1,0:T(8,128)S(1)} %scatter_fusion), channel_id=1, source_target_pairs={{1,0},{2,1},{3,2},{4,3},{5,4},{6,5},{7,6},{8,7},{9,8},{10,9},{11,1... | collective-permute-start | bytes 589832 | tf_op jit(solution)/shard_map/ppermute | solution.py:17
  20.4 22.5 %collective-permute-start.1 = (f32[4,6,16,128]{3,2,1,0:T(8,128)S(1)}, f32[4,6,16,128]{3,2,1,0:T(8,128)S(1)}, u32[]{:S(2)}, u32[]{:S(2)}) collective-permute-start(f32[4,6,16,128]{3,2,1,0:T(8,128)S(1)} %scatter_fusion.1), channel_id=1, source_target_pairs={{0,1},{1,2},{2,3},{3,4},{4,5},{5,6},{6,7},{7,8},{8,9},{9,10},{10,1... | collective-permute-start | bytes 589832 | tf_op jit(solution)/shard_map/ppermute | solution.py:17
  22.8 5.7 %copy-start.21 = (s32[16]{0:T(128)}, s32[16]{0:T(128)S(1)}, u32[]{:S(2)}) copy-start(s32[16]{0:T(128)S(1)} %fusion.194) | copy-start | bytes 196
  23.9 20.5 %collective-permute-start.3 = (f32[1,6,16,128]{3,2,1,0:T(8,128)S(1)}, f32[1,6,16,128]{3,2,1,0:T(8,128)S(1)}, u32[]{:S(2)}, u32[]{:S(2)}) collective-permute-start(f32[1,6,16,128]{3,2,1,0:T(8,128)S(1)} %bitcast.986), channel_id=1, source_target_pairs={{0,16},{16,32},{32,48},{48,64},{64,80},{80,96},{96,112},{112,128},... | collective-permute-start | bytes 147464 | tf_op jit(solution)/shard_map/ppermute | solution.py:17
  28.5 16.0 %collective-permute-start.2 = (f32[1,6,16,128]{3,2,1,0:T(8,128)S(1)}, f32[1,6,16,128]{3,2,1,0:T(8,128)S(1)}, u32[]{:S(2)}, u32[]{:S(2)}) collective-permute-start(f32[1,6,16,128]{3,2,1,0:T(8,128)S(1)} %bitcast.987), channel_id=1, source_target_pairs={{16,0},{32,16},{48,32},{64,48},{80,64},{96,80},{112,96},{128,112},... | collective-permute-start | bytes 147464 | tf_op jit(solution)/shard_map/ppermute | solution.py:17
  34.1 2.7 %copy-start = (f32[4,6,16,16,128]{4,3,2,1,0:T(8,128)S(1)}, f32[4,6,16,16,128]{4,3,2,1,0:T(8,128)}, u32[]{:S(2)}) copy-start(f32[4,6,16,16,128]{4,3,2,1,0:T(8,128)} %param.18) | copy-start | bytes 9437188
  37.9 2.8 %copy-start.35 = (s32[4,4]{1,0:T(4,128)S(1)}, s32[4,4]{1,0:T(4,128)}, u32[]{:S(2)}) copy-start(s32[4,4]{1,0:T(4,128)} %param.22) | copy-start | bytes 196
  40.6 2.3 copy-start.10
  40.6 3.8 %copy-start.29 = (pred[4,4]{1,0:T(4,128)(4,1)}, pred[4,4]{1,0:T(4,128)(4,1)S(1)}, u32[]{:S(2)}) copy-start(pred[4,4]{1,0:T(4,128)(4,1)S(1)} %get-tuple-element.328) | copy-start | bytes 52
  40.6 3.8 %copy-start.31 = (pred[4,4]{1,0:T(4,128)(4,1)}, pred[4,4]{1,0:T(4,128)(4,1)S(1)}, u32[]{:S(2)}) copy-start(pred[4,4]{1,0:T(4,128)(4,1)S(1)} %get-tuple-element.466) | copy-start | bytes 52
  40.7 3.8 %copy-start.33 = (pred[4,4]{1,0:T(4,128)(4,1)}, pred[4,4]{1,0:T(4,128)(4,1)S(1)}, u32[]{:S(2)}) copy-start(pred[4,4]{1,0:T(4,128)(4,1)S(1)} %and_and_fusion.2) | copy-start | bytes 52
  40.7 5.9 %copy-start.23 = (pred[4,4]{1,0:T(4,128)(4,1)}, pred[4,4]{1,0:T(4,128)(4,1)S(1)}, u32[]{:S(2)}) copy-start(pred[4,4]{1,0:T(4,128)(4,1)S(1)} %broadcast_compare_fusion.3) | copy-start | bytes 52
  40.7 2.2 copy-start.11
  40.8 2.1 copy-start.12
  152.6 3.3 %copy-start.18 = (s32[16]{0:T(128)S(1)}, s32[16]{0:T(128)}, u32[]{:S(2)}) copy-start(s32[16]{0:T(128)} %copy-done.17) | copy-start | bytes 196
  153.7 6.8 %copy-start.22 = (s32[16]{0:T(128)S(1)}, s32[16]{0:T(128)}, u32[]{:S(2)}) copy-start(s32[16]{0:T(128)} %copy-done.21) | copy-start | bytes 196
  153.8 18.4 %collective-permute-start.5 = (f32[4,6,16,128]{3,2,1,0:T(8,128)S(1)}, f32[4,6,16,128]{3,2,1,0:T(8,128)S(1)}, u32[]{:S(2)}, u32[]{:S(2)}) collective-permute-start(f32[4,6,16,128]{3,2,1,0:T(8,128)S(1)} %scatter_fusion.5), channel_id=1, source_target_pairs={{0,1},{1,2},{2,3},{3,4},{4,5},{5,6},{6,7},{7,8},{8,9},{9,10},{10,1... | collective-permute-start | bytes 589832 | tf_op jit(solution)/shard_map/ppermute | solution.py:17
  157.0 8.0 %copy-start.26 = (s32[16]{0:T(128)S(1)}, s32[16]{0:T(128)}, u32[]{:S(2)}) copy-start(s32[16]{0:T(128)} %copy-done.25) | copy-start | bytes 196
  157.1 16.7 %collective-permute-start.4 = (f32[4,6,16,128]{3,2,1,0:T(8,128)S(1)}, f32[4,6,16,128]{3,2,1,0:T(8,128)S(1)}, u32[]{:S(2)}, u32[]{:S(2)}) collective-permute-start(f32[4,6,16,128]{3,2,1,0:T(8,128)S(1)} %scatter_fusion.4), channel_id=1, source_target_pairs={{1,0},{2,1},{3,2},{4,3},{5,4},{6,5},{7,6},{8,7},{9,8},{10,9},{11,1... | collective-permute-start | bytes 589832 | tf_op jit(solution)/shard_map/ppermute | solution.py:17
  161.6 13.8 %collective-permute-start.7 = (f32[1,6,16,128]{3,2,1,0:T(8,128)S(1)}, f32[1,6,16,128]{3,2,1,0:T(8,128)S(1)}, u32[]{:S(2)}, u32[]{:S(2)}) collective-permute-start(f32[1,6,16,128]{3,2,1,0:T(8,128)S(1)} %bitcast.985), channel_id=1, source_target_pairs={{0,16},{16,32},{32,48},{48,64},{64,80},{80,96},{96,112},{112,128},... | collective-permute-start | bytes 147464 | tf_op jit(solution)/shard_map/ppermute | solution.py:17
  166.1 9.3 %collective-permute-start.6 = (f32[1,6,16,128]{3,2,1,0:T(8,128)S(1)}, f32[1,6,16,128]{3,2,1,0:T(8,128)S(1)}, u32[]{:S(2)}, u32[]{:S(2)}) collective-permute-start(f32[1,6,16,128]{3,2,1,0:T(8,128)S(1)} %bitcast.984), channel_id=1, source_target_pairs={{16,0},{32,16},{48,32},{64,48},{80,64},{96,80},{112,96},{128,112},... | collective-permute-start | bytes 147464 | tf_op jit(solution)/shard_map/ppermute | solution.py:17
  172.1 3.3 %copy-start.28 = (pred[4,4]{1,0:T(4,128)(4,1)S(1)}, pred[4,4]{1,0:T(4,128)(4,1)}, u32[]{:S(2)}) copy-start(pred[4,4]{1,0:T(4,128)(4,1)} %copy-done.27) | copy-start | bytes 52
  172.1 3.3 %copy-start.30 = (pred[4,4]{1,0:T(4,128)(4,1)S(1)}, pred[4,4]{1,0:T(4,128)(4,1)}, u32[]{:S(2)}) copy-start(pred[4,4]{1,0:T(4,128)(4,1)} %copy-done.29) | copy-start | bytes 52
  172.2 3.3 %copy-start.32 = (pred[4,4]{1,0:T(4,128)(4,1)S(1)}, pred[4,4]{1,0:T(4,128)(4,1)}, u32[]{:S(2)}) copy-start(pred[4,4]{1,0:T(4,128)(4,1)} %copy-done.31) | copy-start | bytes 52
  172.2 3.3 %copy-start.34 = (pred[4,4]{1,0:T(4,128)(4,1)S(1)}, pred[4,4]{1,0:T(4,128)(4,1)}, u32[]{:S(2)}) copy-start(pred[4,4]{1,0:T(4,128)(4,1)} %copy-done.33) | copy-start | bytes 52
  (13 other events, 13.5 us)
Sparse Core Ops, SparseCore 0:
  40.7 103.3 all-gather.1
